TPU v7x, 32 devices: a whole 2x2x4 slice. The times are simulated.
32 devices in a mesh: head: 2 (over x), tok: 16 (over z, y, core).
Axes of the slice: x: 2, y: 2, z: 4, core: 2. Of those that a mesh axis runs over, the one named last changes fastest.
Arguments:
- queries: bfloat16 [3072, 1024], P('tok', 'head'), may hold values from -512 to 512
- keys: bfloat16 [3072, 1024], P('tok', 'head'), may hold values from -8 to 8
- values: bfloat16 [3072, 1024], P('tok', 'head'), may hold values from -6 to 6
- out_grad: bfloat16 [3072, 1024], P('tok', 'head'), may hold values from -6 to 6
- w_query: bfloat16 [1024, 1024], P(None, 'head'), may hold values from -0.1875 to 0.1875
- w_key: bfloat16 [1024, 1024], P(None, 'head'), may hold values from -0.1875 to 0.1875
- w_value: bfloat16 [1024, 1024], P(None, 'head'), may hold values from -0.1875 to 0.1875
- w_out: bfloat16 [1024, 1024], P('head'), may hold values from -0.1875 to 0.1875
- page_cluster: int32 [96], replicated, may hold values from 0 to 15, as said below
Outputs:
- input_grad: bfloat16 [3072, 1024], P('tok', 'head')
Inputs may be any that keep to these rules, and one draw needn't show every extreme that they name: `page_cluster`: the 6 pages k * 6 to k * 6 + 5, for each k, name distinct clusters. No cluster is named by more than 8 pages, and some cluster by exactly 8.
All inputs are finite; a program needn't handle non-finite values.
Results may differ from a plain program's by a relative error of at most 0.014.
Values may be sent and summed in bfloat16 or wider, within the bound.
A program may use at most 64 MiB of HBM per device.

v0:
```python
import jax
import jax.numpy as jnp
from jax import lax
from jax.sharding import PartitionSpec as P

HEAD_DIM = 128
PAGE = 32


def per_device(queries, keys, values, out_grad, w_query, w_key, w_value, w_out, page_cluster):
    tok_rows, head_cols = queries.shape
    pages_here = tok_rows // PAGE
    heads_here = head_cols // HEAD_DIM
    peers = lax.axis_size("tok")
    myself = lax.axis_index("tok")
    page_total = page_cluster.shape[0]
    slot_count = peers // 2
    cluster_rows = slot_count * PAGE
    score_scale = HEAD_DIM ** (-0.5)
    grad_heads = jnp.einsum(
        "td,hd->th",
        lax.all_gather(out_grad, "head", axis=1, tiled=True),
        w_out,
        preferred_element_type=jnp.float32,
    ).astype(jnp.bfloat16)
    page_order = jnp.arange(page_total, dtype=jnp.int32)
    peer_order = jnp.arange(peers, dtype=jnp.int32)
    cluster_onehot = (page_cluster[:, None] == peer_order[None, :]).astype(jnp.int32)
    running_count = jnp.cumsum(cluster_onehot, axis=0) - cluster_onehot
    page_rank = jnp.sum(running_count * cluster_onehot, axis=1)
    my_clusters = lax.dynamic_slice_in_dim(page_cluster, myself * pages_here, pages_here)
    going = my_clusters[None, :] == peer_order[:, None]
    going_any = jnp.any(going, axis=1)
    going_index = jnp.sum(
        going.astype(jnp.int32) * jnp.arange(pages_here, dtype=jnp.int32)[None, :], axis=1
    )

    def outgoing(matrix):
        paged = matrix.reshape(pages_here, PAGE, matrix.shape[1])
        picked = jnp.take(paged, going_index, axis=0)
        return jnp.where(going_any[:, None, None], picked, jnp.zeros_like(picked))

    arrived = (
        lax.all_to_all(outgoing(queries), "tok", split_axis=0, concat_axis=0, tiled=True),
        lax.all_to_all(outgoing(keys), "tok", split_axis=0, concat_axis=0, tiled=True),
        lax.all_to_all(outgoing(values), "tok", split_axis=0, concat_axis=0, tiled=True),
        lax.all_to_all(outgoing(grad_heads), "tok", split_axis=0, concat_axis=0, tiled=True),
    )
    slot_order = jnp.arange(slot_count, dtype=jnp.int32)
    slot_hit = (page_cluster[None, :] == myself) & (page_rank[None, :] == slot_order[:, None])
    filled = jnp.any(slot_hit, axis=1)
    slot_page = jnp.sum(slot_hit.astype(jnp.int32) * page_order[None, :], axis=1)
    slot_source = slot_page // pages_here

    def assemble(matrix):
        picked = jnp.take(matrix, slot_source, axis=0)
        picked = jnp.where(filled[:, None, None], picked, jnp.zeros_like(picked))
        return picked.reshape(cluster_rows, heads_here, HEAD_DIM)

    slot_query = assemble(arrived[0])
    slot_keys = assemble(arrived[1])
    slot_values = assemble(arrived[2])
    slot_grads = assemble(arrived[3])
    inner_index = jnp.arange(PAGE, dtype=jnp.int32)
    key_pos = (slot_page[:, None] * PAGE + inner_index[None, :]).reshape(cluster_rows)
    key_live = jnp.broadcast_to(filled[:, None], (slot_count, PAGE)).reshape(cluster_rows)
    key_order = jnp.arange(cluster_rows, dtype=jnp.int32)
    block_rows = min(512, cluster_rows)
    dkey_sum = jnp.zeros((cluster_rows, heads_here, HEAD_DIM), jnp.float32)
    dvalue_sum = jnp.zeros((cluster_rows, heads_here, HEAD_DIM), jnp.float32)
    query_parts = []
    for block_index in range(cluster_rows // block_rows):
        first_row = block_index * block_rows
        last_row = first_row + block_rows
        part_query = slot_query[first_row:last_row]
        part_grads = slot_grads[first_row:last_row]
        row_pos = key_pos[first_row:last_row]
        row_order = key_order[first_row:last_row]
        allowed = key_live[None, :] & (key_pos[None, :] <= row_pos[:, None]) | (
            key_order[None, :] == row_order[:, None]
        )
        score = (
            jnp.einsum("qhd,khd->hqk", part_query, slot_keys, preferred_element_type=jnp.float32)
            * score_scale
        )
        score = jnp.where(allowed[None], score, -1e30)
        row_max = jnp.max(score, axis=2, keepdims=True)
        raised = jnp.where(allowed[None], jnp.exp(score - row_max), 0.0)
        weights = raised / jnp.sum(raised, axis=2, keepdims=True)
        weights_half = weights.astype(jnp.bfloat16)
        grad_weights = jnp.einsum(
            "qhd,khd->hqk", part_grads, slot_values, preferred_element_type=jnp.float32
        )
        row_delta = jnp.sum(weights * grad_weights, axis=2, keepdims=True)
        grad_score = (weights * (grad_weights - row_delta)).astype(jnp.bfloat16)
        grad_query = (
            jnp.einsum("hqk,khd->qhd", grad_score, slot_keys, preferred_element_type=jnp.float32)
            * score_scale
        )
        query_parts.append(grad_query.astype(jnp.bfloat16))
        dkey_sum = dkey_sum + jnp.einsum(
            "hqk,qhd->khd", grad_score, part_query, preferred_element_type=jnp.float32
        )
        dvalue_sum = dvalue_sum + jnp.einsum(
            "hqk,qhd->khd", weights_half, part_grads, preferred_element_type=jnp.float32
        )
    slot_dquery = jnp.concatenate(query_parts, axis=0).reshape(cluster_rows, head_cols)
    slot_dkey = (dkey_sum * score_scale).astype(jnp.bfloat16).reshape(cluster_rows, head_cols)
    slot_dvalue = dvalue_sum.astype(jnp.bfloat16).reshape(cluster_rows, head_cols)
    back_hit = (slot_source[None, :] == peer_order[:, None]) & filled[None, :]
    back_any = jnp.any(back_hit, axis=1)
    back_slot = jnp.sum(back_hit.astype(jnp.int32) * slot_order[None, :], axis=1)
    share_rows = w_query.shape[0] // lax.axis_size("head")
    total = jnp.einsum("dh,th->dt", w_query, slot_dquery, preferred_element_type=jnp.float32)
    total = total + jnp.einsum("dh,th->dt", w_key, slot_dkey, preferred_element_type=jnp.float32)
    total = total + jnp.einsum(
        "dh,th->dt", w_value, slot_dvalue, preferred_element_type=jnp.float32
    )
    column_share = lax.psum_scatter(
        total.astype(jnp.bfloat16), "head", scatter_dimension=0, tiled=True
    )
    column_share = column_share.reshape(share_rows, slot_count, PAGE)
    picked = jnp.take(column_share, back_slot, axis=1)
    picked = jnp.where(back_any[None, :, None], picked, jnp.zeros_like(picked))
    returned = lax.all_to_all(picked, "tok", split_axis=1, concat_axis=1, tiled=True)
    input_grad = jnp.take(returned, my_clusters, axis=1).reshape(share_rows, tok_rows).T
    return input_grad


def solution(mesh):
    placed = (
        P("tok", "head"),
        P("tok", "head"),
        P("tok", "head"),
        P("tok", "head"),
        P(None, "head"),
        P(None, "head"),
        P(None, "head"),
        P("head", None),
        P(),
    )
    return jax.shard_map(
        per_device, mesh=mesh, in_specs=placed, out_specs=P("tok", "head"), check_vma=False
    )
```

profile of v0, /device:TPU:0, one launch (start us, length us, event | category | flops | bytes accessed | tf_op | source)
XLA Modules:
  0.0 150.0 jit_solution(11652533963918098453)
XLA Ops:
  6.5 0.8 compare_and_fusion.3
  7.4 0.1 select_reduce_fusion.1
  7.5 0.1 fusion.14
  7.6 8.8 %all_gather.3 = bf16[192,1024]{1,0:T(8,128)(2,1)S(1)} all-gather(bf16[192,512]{1,0:T(8,128)(2,1)} %param.16), channel_id=1, replica_groups=mesh['head'=2,'tok'=16] {'head'}, dimensions={1}, use_global_device_ids=true | all-gather | bytes 589824 | tf_op jit(solution)/shard_map/all_gather | solution.py:22
  16.3 1.8 %convolution_convert_fusion.1 = bf16[192,512]{1,0:T(8,128)(2,1)S(1)} fusion(bf16[192,1024]{1,0:T(8,128)(2,1)S(1)} %all_gather.3, bf16[512,1024]{1,0:T(8,128)(2,1)} %param.20), kind=kOutput, calls=%fused_computation.25 | convolution fusion | flops 201424896 | bytes 1638400 | tf_op jit(solution)/shard_map/td,hd->th/dot_general | solution.py:20
  18.1 0.0 copy-start.2
  18.1 0.6 gather_fusion.6
  18.7 0.0 copy-start.3
  18.7 0.6 gather_fusion.2
  19.3 0.6 gather_fusion.4
  19.9 0.6 gather_fusion.8
  20.5 1.3 select_select_fusion.2
  21.8 20.2 %all_to_all.25 = bf16[16,32,512]{2,1,0:T(8,128)(2,1)S(1)} all-to-all(bf16[16,32,512]{2,1,0:T(8,128)(2,1)S(1)} %get-tuple-element.18), channel_id=1, replica_groups=mesh['head'=2,'tok'=16] {'tok'}, dimensions={0} | all-to-all | bytes 1048576 | tf_op jit(solution)/shard_map/all_to_all | solution.py:45
  42.0 18.4 %all_to_all.26 = bf16[16,32,512]{2,1,0:T(8,128)(2,1)S(1)} all-to-all(bf16[16,32,512]{2,1,0:T(8,128)(2,1)S(1)} %get-tuple-element.16), channel_id=1, replica_groups=mesh['head'=2,'tok'=16] {'tok'}, dimensions={0} | all-to-all | bytes 1048576 | tf_op jit(solution)/shard_map/all_to_all | solution.py:47
  60.4 4.2 %all-to-all-start.3 = ((bf16[16,32,512]{2,1,0:T(8,128)(2,1)}), bf16[16,32,512]{2,1,0:T(8,128)(2,1)S(1)}, u32[]{:S(2)}, u32[]{:S(2)}) async-start(bf16[16,32,512]{2,1,0:T(8,128)(2,1)} %get-tuple-element.17), calls=%async_computation.3 | async-start | bytes 1048576 | tf_op jit(solution)/shard_map/all_to_all | solution.py:46
  64.6 0.1 fusion.13
  64.6 0.1 reduce_window_sum.11
  64.8 0.2 select_reduce_fusion
  65.0 0.1 fusion.16
  65.1 0.1 broadcast_in_dim.151
  65.2 0.1 and.66
  65.3 0.1 select_reduce_fusion.3
  65.4 13.4 %all-to-all-done.3 = bf16[16,32,512]{2,1,0:T(8,128)(2,1)S(1)} async-done(((bf16[16,32,512]{2,1,0:T(8,128)(2,1)}), bf16[16,32,512]{2,1,0:T(8,128)(2,1)S(1)}, u32[]{:S(2)}, u32[]{:S(2)}) %all-to-all-start.3) | async-done | bytes 524320 | tf_op jit(solution)/shard_map/all_to_all | solution.py:46
  78.8 4.2 %all-to-all-start.1 = ((bf16[16,32,512]{2,1,0:T(8,128)(2,1)}), bf16[16,32,512]{2,1,0:T(8,128)(2,1)S(1)}, u32[]{:S(2)}, u32[]{:S(2)}) async-start(bf16[16,32,512]{2,1,0:T(8,128)(2,1)} %get-tuple-element.15), calls=%async_computation.1 | async-start | bytes 1048576 | tf_op jit(solution)/shard_map/all_to_all | solution.py:44
  83.0 0.0 reduce-scatter.2.cloned.1.call-start
  83.0 0.1 iota_add_fusion
  83.1 0.1 add.73
  83.2 0.1 fusion.12
  83.4 0.6 gather_fusion.3
  84.0 0.6 gather_fusion.7
  84.5 0.6 gather_fusion.9
  85.1 12.2 %all-to-all-done.1 = bf16[16,32,512]{2,1,0:T(8,128)(2,1)S(1)} async-done(((bf16[16,32,512]{2,1,0:T(8,128)(2,1)}), bf16[16,32,512]{2,1,0:T(8,128)(2,1)S(1)}, u32[]{:S(2)}, u32[]{:S(2)}) %all-to-all-start.1) | async-done | bytes 524320 | tf_op jit(solution)/shard_map/all_to_all | solution.py:44
  97.3 0.6 gather_fusion.5
  97.8 0.2 select_select_fusion.6
  98.0 0.1 reshape.186
  98.1 0.2 copy.33
  98.3 0.1 reshape.188
  98.3 0.2 copy.35
  98.5 0.1 reshape.190
  98.6 0.2 copy.37
  98.8 0.1 reshape.192
  98.9 0.6 fusion.23
  99.5 0.9 convolution_convert_fusion
  100.4 0.3 multiply_reduce_fusion
  100.7 0.2 multiply_convert_fusion
  100.9 0.3 fusion.8
  101.2 0.2 fusion.7
  101.5 0.5 fusion.24
  101.9 0.7 copy-done.4
  102.7 0.5 convolution_add_fusion.1
  103.2 0.7 copy-done.5
  103.9 1.3 fusion.6
  105.2 0.0 reduce-scatter.2.cloned.1.call-update
  105.2 0.1 select_reduce_fusion.2
  105.3 0.1 fusion.18
  105.4 14.1 %reduce-scatter.2.cloned.1.call-done = bf16[512,256]{0,1:T(8,128)(2,1)} async-done(((bf16[1024,256]{0,1:T(8,128)(2,1)}), bf16[512,256]{0,1:T(8,128)(2,1)}) %reduce-scatter.2.cloned.1.call-update) | async-done | bytes 262160 | tf_op jit(solution)/shard_map/reduce_scatter | solution.py:119
  119.5 1.5 %gather_fusion = bf16[16,512,32]{1,2,0:T(8,128)(2,1)S(1)} fusion(bf16[512,8,32]{0,2,1:T(8,128)(2,1)} %bitcast.45, s32[1024]{0:T(1024)S(1)} %pad_clamp_fusion.1), kind=kCustom, calls=%fused_computation.8 | custom fusion | bytes 1048640 | tf_op jit(solution)/shard_map/jit(_take)/gather | solution.py:123
  121.0 0.9 select_bitcast_fusion
  122.0 5.6 %all-to-all-start.4 = ((bf16[512,16,32]{0,2,1:T(8,128)(2,1)}), bf16[512,16,32]{0,2,1:T(8,128)(2,1)S(1)}, u32[]{:S(2)}, u32[]{:S(2)}) async-start(bf16[512,16,32]{0,2,1:T(8,128)(2,1)} %select_bitcast_fusion), calls=%async_computation.5 | async-start | bytes 1048576 | tf_op jit(solution)/shard_map/all_to_all | solution.py:125
  127.6 0.1 broadcast_in_dim.144
  127.7 0.1 broadcast_in_dim.145
  127.8 14.1 %all-to-all-done.4 = bf16[512,16,32]{0,2,1:T(8,128)(2,1)S(1)} async-done(((bf16[512,16,32]{0,2,1:T(8,128)(2,1)}), bf16[512,16,32]{0,2,1:T(8,128)(2,1)S(1)}, u32[]{:S(2)}, u32[]{:S(2)}) %all-to-all-start.4) | async-done | bytes 524320 | tf_op jit(solution)/shard_map/all_to_all | solution.py:125
  141.9 0.6 gather_fusion.1
  142.4 0.8 bitcast_select_fusion
  (23 shorter events, 0.1 us)
Async XLA Ops:
  6.5 94.9 %copy-start = (bf16[1024,512]{1,0:T(8,128)(2,1)S(1)}, bf16[1024,512]{1,0:T(8,128)(2,1)}, u32[]{:S(2)}) copy-start(bf16[1024,512]{1,0:T(8,128)(2,1)} %param.17) | copy-start | bytes 3145732
  16.3 2.4 %copy-start.1 = (bf16[192,512]{1,0:T(8,128)(2,1)S(1)}, bf16[192,512]{1,0:T(8,128)(2,1)}, u32[]{:S(2)}) copy-start(bf16[192,512]{1,0:T(8,128)(2,1)} %param.14) | copy-start | bytes 589828
  18.1 1.2 copy-start.2
  18.7 1.2 copy-start.3
  42.0 22.5 %copy-start.6 = (s32[96]{0:T(128)S(1)}, s32[96]{0:T(128)}, u32[]{:S(2)}) copy-start(s32[96]{0:T(128)} %param.21) | copy-start | bytes 1156
  60.4 18.4 %all-to-all-start.3 = ((bf16[16,32,512]{2,1,0:T(8,128)(2,1)}), bf16[16,32,512]{2,1,0:T(8,128)(2,1)S(1)}, u32[]{:S(2)}, u32[]{:S(2)}) async-start(bf16[16,32,512]{2,1,0:T(8,128)(2,1)} %get-tuple-element.17), calls=%async_computation.3 | async-start | bytes 1048576 | tf_op jit(solution)/shard_map/all_to_all | solution.py:46
  78.8 18.4 %all-to-all-start.1 = ((bf16[16,32,512]{2,1,0:T(8,128)(2,1)}), bf16[16,32,512]{2,1,0:T(8,128)(2,1)S(1)}, u32[]{:S(2)}, u32[]{:S(2)}) async-start(bf16[16,32,512]{2,1,0:T(8,128)(2,1)} %get-tuple-element.15), calls=%async_computation.1 | async-start | bytes 1048576 | tf_op jit(solution)/shard_map/all_to_all | solution.py:44
  83.0 36.5 %reduce-scatter.2.cloned.1.call-start = ((), (), s32[]{:S(2)}) async-start(), calls=%async_computation.6 | async-start | bytes 786432 | tf_op jit(solution)/shard_map/reduce_scatter | solution.py:119
  101.4 1.2 copy-start.4
  102.7 1.2 copy-start.5
  122.0 19.9 %all-to-all-start.4 = ((bf16[512,16,32]{0,2,1:T(8,128)(2,1)}), bf16[512,16,32]{0,2,1:T(8,128)(2,1)S(1)}, u32[]{:S(2)}, u32[]{:S(2)}) async-start(bf16[512,16,32]{0,2,1:T(8,128)(2,1)} %select_bitcast_fusion), calls=%async_computation.5 | async-start | bytes 1048576 | tf_op jit(solution)/shard_map/all_to_all | solution.py:125
Sparse Core Ops, SparseCore 0:
  105.3 14.1 reduce-scatter.1
where the time goes:
time: 151 us; the launch traced here: 150 us
  waiting for transfers between devices  53.8 us (36%)
  blocking collectives  47.3 us (31%)
  starting transfers between devices  14 us (9%)
  between operations  13.7 us (9%)
  local copies, waits for them, and re-layouts  9.34 us (6%)
  matrix products  6.38 us (4%)
  other arithmetic  5.46 us (4%)
    all_to_all x1, blocking collectives, per_device(): lax.all_to_all(outgoing(keys), 'tok', split_axis=0, concat_axis=0, tiled=...  20.2 us
    all_to_all x1, blocking collectives, per_device(): lax.all_to_all(outgoing(grad_heads), 'tok', split_axis=0, concat_axis=0,...  18.4 us
    all_to_all x1, waiting for transfers between devices, per_device(): lax.all_to_all(picked, 'tok', split_axis=1, concat_axis=1, tiled=True)  14.1 us
    reduce_scatter x1, waiting for transfers between devices, per_device(): lax.psum_scatter(total.astype(jnp.bfloat16), 'head', scatter_dimension=0,...  14.1 us
    all_to_all x1, waiting for transfers between devices, per_device(): lax.all_to_all(outgoing(values), 'tok', split_axis=0, concat_axis=0, tile...  13.4 us
    all_to_all x1, waiting for transfers between devices, per_device(): lax.all_to_all(outgoing(queries), 'tok', split_axis=0, concat_axis=0, til...  12.2 us
    all_gather x1, blocking collectives, per_device(): lax.all_gather(out_grad, 'head', axis=1, tiled=True)  8.79 us
    all_to_all x1, starting transfers between devices, per_device(): lax.all_to_all(picked, 'tok', split_axis=1, concat_axis=1, tiled=True)  5.62 us
  transfers between devices with their start and end apart: 4, of which 4 were waited for; matrix products, arithmetic and copies ran while one was open for 2% of the time, Pallas kernels for 0%

commit v1 on v0

--- a/solution.py
+++ b/solution.py
@@ -1,6 +1,10 @@
+import functools
+
 import jax
 import jax.numpy as jnp
 from jax import lax
+from jax.experimental import pallas as pl
+from jax.experimental.pallas import tpu as pltpu
 from jax.sharding import PartitionSpec as P
 
 HEAD_DIM = 128
@@ -127,6 +131,296 @@
     return input_grad
 
 
+MESH = pl.DeviceIdType.MESH
+NT = (((1,), (1,)), ((), ()))
+TN = (((0,), (0,)), ((), ()))
+
+
+def dot(a, b, dims):
+    return lax.dot_general(a, b, dims, preferred_element_type=jnp.float32)
+
+
+def whole_kernel(
+    sizes, slot_ref, place_ref, q_ref, k_ref, v_ref, og_ref, wq_ref, wk_ref, wv_ref, wo_ref, out_ref,
+    og_mine, og_other, wq_vm, wk_vm, wv_vm, wo_vm, grads, all_q, all_k, all_v, all_g,
+    slot_q, slot_k, slot_v, done_q, done_k, done_v, ret_q, ret_k, ret_v, part_out, part_in,
+    load_sem, swap_send, swap_recv, fwd_send, fwd_recv, ret_send, ret_recv,
+):
+    peers, pages, heads, slots = sizes
+    width = heads * HEAD_DIM
+    rows = pages * PAGE
+    scale = HEAD_DIM ** (-0.5)
+    me = lax.axis_index("tok")
+    group = lax.axis_index("head")
+    other = 1 - group
+    owners = [peers // 4 + head * (peers // 2) // heads for head in range(heads)]
+
+    loads = [
+        pltpu.make_async_copy(og_ref, og_mine, load_sem.at[0]),
+        pltpu.make_async_copy(wo_ref, wo_vm, load_sem.at[1]),
+        pltpu.make_async_copy(wq_ref, wq_vm, load_sem.at[2]),
+        pltpu.make_async_copy(wk_ref, wk_vm, load_sem.at[3]),
+        pltpu.make_async_copy(wv_ref, wv_vm, load_sem.at[4]),
+    ]
+    for load in loads:
+        load.start()
+
+    barrier = pltpu.get_barrier_semaphore()
+    pl.semaphore_signal(barrier, inc=1, device_id={"head": other}, device_id_type=MESH)
+    for peer in range(peers):
+        @pl.when(me != peer)
+        def _():
+            pl.semaphore_signal(barrier, inc=1, device_id={"tok": peer}, device_id_type=MESH)
+    zero_page = jnp.zeros((PAGE, HEAD_DIM), jnp.bfloat16)
+    for full in (all_q, all_k, all_v, all_g):
+        full[peers * pages] = zero_page
+    pl.semaphore_wait(barrier, peers)
+
+    og_swap = pltpu.make_async_remote_copy(
+        src_ref=og_ref, dst_ref=og_other, send_sem=swap_send.at[0], recv_sem=swap_recv.at[0],
+        device_id={"head": other}, device_id_type=MESH,
+    )
+    og_swap.start()
+
+    fulls = (all_q, all_k, all_v, all_g)
+    sources = (q_ref, k_ref, v_ref, grads)
+
+    def forward(tensor, head):
+        piece = sources[tensor].at[:, :, pl.ds(head * HEAD_DIM, HEAD_DIM)]
+        spot = fulls[tensor].at[pl.ds(me * pages, pages)]
+        local = pltpu.make_async_copy(piece, spot, fwd_recv.at[tensor, me])
+        remote = pltpu.make_async_remote_copy(
+            src_ref=piece, dst_ref=spot, send_sem=fwd_send.at[tensor, head],
+            recv_sem=fwd_recv.at[tensor, me], device_id={"tok": owners[head]}, device_id_type=MESH,
+        )
+        return local, remote
+
+    def send_forward(tensor):
+        for head in range(heads):
+            local, remote = forward(tensor, head)
+
+            @pl.when(me == owners[head])
+            def _():
+                local.start()
+
+            @pl.when(me != owners[head])
+            def _():
+                remote.start()
+
+    for tensor in range(3):
+        send_forward(tensor)
+
+    loads[0].wait()
+    loads[1].wait()
+    here = pl.ds(pl.multiple_of(group * width, HEAD_DIM), width)
+    there = pl.ds(pl.multiple_of(other * width, HEAD_DIM), width)
+    grad_sum = dot(og_mine[...].reshape(rows, width), wo_vm[:, here], NT)
+    og_swap.wait()
+    grad_sum = grad_sum + dot(og_other[...].reshape(rows, width), wo_vm[:, there], NT)
+    grads[...] = grad_sum.astype(jnp.bfloat16).reshape(pages, PAGE, width)
+    send_forward(3)
+
+    slot_sets = (slot_q, slot_k, slot_v)
+    done_sets = (done_q, done_k, done_v)
+    ret_sets = (ret_q, ret_k, ret_v)
+    cluster_rows = slots * PAGE
+
+    def give_back(tensor, head, peer):
+        piece = done_sets[tensor].at[pl.ds(peer * pages, pages)]
+        spot = ret_sets[tensor].at[:, :, pl.ds(head * HEAD_DIM, HEAD_DIM)]
+        local = pltpu.make_async_copy(piece, spot, ret_recv.at[tensor, head])
+        remote = pltpu.make_async_remote_copy(
+            src_ref=piece, dst_ref=spot, send_sem=ret_send.at[tensor, peer],
+            recv_sem=ret_recv.at[tensor, head], device_id={"tok": peer}, device_id_type=MESH,
+        )
+        return local, remote
+
+    def own_head(head):
+        for tensor in range(4):
+            for peer in range(peers):
+                piece = sources[tensor].at[:, :, pl.ds(head * HEAD_DIM, HEAD_DIM)]
+                spot = fulls[tensor].at[pl.ds(peer * pages, pages)]
+                if peer == owners[head]:
+                    pltpu.make_async_copy(piece, spot, fwd_recv.at[tensor, peer]).wait()
+                else:
+                    pltpu.make_async_remote_copy(
+                        src_ref=piece, dst_ref=spot, send_sem=fwd_send.at[tensor, head],
+                        recv_sem=fwd_recv.at[tensor, peer], device_id={"tok": peer}, device_id_type=MESH,
+                    ).wait_recv()
+
+    for head in range(heads):
+        @pl.when(me == owners[head])
+        def _():
+            own_head(head)
+
+    is_owner = functools.reduce(lambda a, b: a | b, [me == owner for owner in owners])
+
+    @pl.when(is_owner)
+    def _():
+        row_index = lax.broadcasted_iota(jnp.int32, (cluster_rows, cluster_rows), 0)
+        col_index = lax.broadcasted_iota(jnp.int32, (cluster_rows, cluster_rows), 1)
+
+        def cluster_step(cluster, carry):
+            picks = [slot_ref[cluster * slots + slot] for slot in range(slots)]
+            query, key, value, grad = [
+                jnp.concatenate([full[pick] for pick in picks], axis=0) for full in fulls
+            ]
+            allowed = col_index <= row_index
+            score = jnp.where(allowed, dot(query, key, NT) * scale, -1e30)
+            row_max = jnp.max(score, axis=1, keepdims=True)
+            raised = jnp.where(allowed, jnp.exp(score - row_max), 0.0)
+            weights = raised * (1.0 / jnp.sum(raised, axis=1, keepdims=True))
+            grad_weights = dot(grad, value, NT)
+            row_delta = jnp.sum(weights * grad_weights, axis=1, keepdims=True)
+            grad_score = (weights * (grad_weights - row_delta)).astype(jnp.bfloat16)
+            dquery = dot(grad_score, key, (((1,), (0,)), ((), ()))) * scale
+            dkey = dot(grad_score, query, TN) * scale
+            dvalue = dot(weights.astype(jnp.bfloat16), grad, TN)
+            spot = pl.ds(cluster * slots, slots)
+            shape = (slots, PAGE, HEAD_DIM)
+            slot_q[spot] = dquery.astype(jnp.bfloat16).reshape(shape)
+            slot_k[spot] = dkey.astype(jnp.bfloat16).reshape(shape)
+            slot_v[spot] = dvalue.astype(jnp.bfloat16).reshape(shape)
+            return carry
+
+        lax.fori_loop(0, peers, cluster_step, 0)
+
+        def page_step(page, carry):
+            place = place_ref[page]
+            for slot_set, done_set in zip(slot_sets, done_sets):
+                done_set[page] = slot_set[place]
+            return carry
+
+        lax.fori_loop(0, peers * pages, page_step, 0)
+
+    def send_back(head):
+        for peer in range(peers):
+            for tensor in range(3):
+                local, remote = give_back(tensor, head, peer)
+                if peer == owners[head]:
+                    local.start()
+                else:
+                    remote.start()
+
+    for head in range(heads):
+        @pl.when(me == owners[head])
+        def _():
+            send_back(head)
+
+    for tensor in range(3):
+        for head in range(heads):
+            local, remote = give_back(tensor, head, owners[head])
+
+            @pl.when(me == owners[head])
+            def _():
+                local.wait()
+
+            @pl.when(me != owners[head])
+            def _():
+                remote.wait_recv()
+
+    for load in loads[2:]:
+        load.wait()
+    grads_in = [ret[...].reshape(rows, width) for ret in ret_sets]
+    weights_in = (wq_vm, wk_vm, wv_vm)
+
+    def partial(half):
+        total = dot(grads_in[0], weights_in[0][half, :], NT)
+        total = total + dot(grads_in[1], weights_in[1][half, :], NT)
+        return (total + dot(grads_in[2], weights_in[2][half, :], NT)).astype(jnp.bfloat16)
+
+    part_out[...] = partial(there)
+    part_swap = pltpu.make_async_remote_copy(
+        src_ref=part_out, dst_ref=part_in, send_sem=swap_send.at[1], recv_sem=swap_recv.at[1],
+        device_id={"head": other}, device_id_type=MESH,
+    )
+    part_swap.start()
+    mine = partial(here).astype(jnp.float32)
+    part_swap.wait()
+    out_ref[...] = (mine + part_in[...].astype(jnp.float32)).astype(jnp.bfloat16)
+
+    for head in range(heads):
+        @pl.when(me != owners[head])
+        def _():
+            for tensor in range(4):
+                forward(tensor, head)[1].wait_send()
+
+        @pl.when(me == owners[head])
+        def _():
+            for peer in range(peers):
+                if peer != owners[head]:
+                    for tensor in range(3):
+                        give_back(tensor, head, peer)[1].wait_send()
+
+
+def gathered_bytes(peers, rows, heads):
+    tokens = peers * rows
+    slot_rows = peers * (peers // 2) * PAGE
+    return (4 * tokens + 3 * slot_rows + 3 * tokens) * HEAD_DIM * 2
+
+
+def per_device_fast(queries, keys, values, out_grad, w_query, w_key, w_value, w_out, page_cluster):
+    rows, width = queries.shape
+    pages = rows // PAGE
+    heads = width // HEAD_DIM
+    peers = lax.axis_size("tok")
+    slots = peers // 2
+    page_total = page_cluster.shape[0]
+    page_order = jnp.arange(page_total, dtype=jnp.int32)
+    same = page_cluster[:, None] == page_cluster[None, :]
+    earlier = page_order[None, :] < page_order[:, None]
+    rank = jnp.sum((same & earlier).astype(jnp.int32), axis=1)
+    place = page_cluster * slots + rank
+    slot_order = jnp.arange(peers * slots, dtype=jnp.int32)
+    hit = place[None, :] == slot_order[:, None]
+    slot_page = page_total + jnp.sum(
+        jnp.where(hit, page_order[None, :] - page_total, 0), axis=1
+    ).astype(jnp.int32)
+    paged = (pages, PAGE, width)
+    half = jnp.bfloat16
+    full = pltpu.VMEM((page_total + 1, PAGE, HEAD_DIM), half)
+    slotted = pltpu.VMEM((peers * slots, PAGE, HEAD_DIM), half)
+    done = pltpu.VMEM((page_total, PAGE, HEAD_DIM), half)
+    small = pltpu.VMEM(paged, half)
+    weight = pltpu.VMEM(w_query.shape, half)
+    any_space = pl.BlockSpec(memory_space=pl.ANY)
+    smem = pl.BlockSpec(memory_space=pltpu.SMEM)
+    return pl.pallas_call(
+        functools.partial(whole_kernel, (peers, pages, heads, slots)),
+        out_shape=jax.ShapeDtypeStruct((rows, width), half),
+        in_specs=[smem, smem] + [any_space] * 8,
+        out_specs=pl.BlockSpec(memory_space=pltpu.VMEM),
+        scratch_shapes=[small, small, weight, weight, weight, pltpu.VMEM(w_out.shape, half), small]
+        + [full] * 4 + [slotted] * 3 + [done] * 3 + [small] * 3
+        + [pltpu.VMEM((rows, width), half)] * 2
+        + [
+            pltpu.SemaphoreType.DMA((5,)),
+            pltpu.SemaphoreType.DMA((2,)),
+            pltpu.SemaphoreType.DMA((2,)),
+            pltpu.SemaphoreType.DMA((4, heads)),
+            pltpu.SemaphoreType.DMA((4, peers)),
+            pltpu.SemaphoreType.DMA((3, peers)),
+            pltpu.SemaphoreType.DMA((3, heads)),
+        ],
+        compiler_params=pltpu.CompilerParams(
+            collective_id=0, has_side_effects=True, vmem_limit_bytes=40 * 1024 * 1024
+        ),
+    )(
+        slot_page, place, queries.reshape(paged), keys.reshape(paged), values.reshape(paged),
+        out_grad.reshape(paged), w_query, w_key, w_value, w_out,
+    )
+
+
+def choose(*arrays):
+    rows, width = arrays[0].shape
+    heads = width // HEAD_DIM
+    peers = lax.axis_size("tok")
+    fits = gathered_bytes(peers, rows, heads) < 24 * 1024 * 1024
+    if lax.axis_size("head") == 2 and heads > 1 and (peers // 2) % heads == 0 and fits:
+        return per_device_fast(*arrays)
+    return per_device(*arrays)
+
+
 def solution(mesh):
     placed = (
         P("tok", "head"),
@@ -140,5 +434,5 @@
         P(),
     )
     return jax.shard_map(
-        per_device, mesh=mesh, in_specs=placed, out_specs=P("tok", "head"), check_vma=False
-    )
+        choose, mesh=mesh, in_specs=placed, out_specs=P("tok", "head"), check_vma=False
+    )

time: 151 us -> 70.5 us (0.47)
  the two profiles are of different devices: /device:TPU:0 before, /device:TPU:13 now
where the time goes in v1:
time: 70.5 us; the launch traced here: 70.1 us
  Pallas kernels  59.9 us (85%)
  local copies, waits for them, and re-layouts  9.93 us (14%)
    pallas_call x1, Pallas kernels, per_device_fast(): pl.pallas_call(functools.partial(whole_kernel, (peers, pages, heads, slot...  59.9 us
    unnamed x19, local copies, waits for them, and re-layouts  9.93 us

profile of v1, /device:TPU:13, one launch (start us, length us, event | category | flops | bytes accessed | tf_op | source)
XLA Modules:
  0.0 70.1 jit_solution(10179892318782007162)
XLA Ops:
  0.0 0.0 copy-start.8
  0.0 0.7 copy-done.8
  0.7 0.2 convert_reduce_fusion
  0.8 0.1 select_reduce_fusion
  1.0 0.0 copy-start
  1.0 1.2 %copy-done = bf16[1024,512]{1,0:T(8,128)(2,1)S(1)} copy-done((bf16[1024,512]{1,0:T(8,128)(2,1)S(1)}, bf16[1024,512]{1,0:T(8,128)(2,1)}, u32[]{:S(2)}) %copy-start) | copy-done | bytes 1048600
  2.2 0.0 copy-start.1
  2.2 1.2 %copy-done.1 = bf16[1024,512]{1,0:T(8,128)(2,1)S(1)} copy-done((bf16[1024,512]{1,0:T(8,128)(2,1)S(1)}, bf16[1024,512]{1,0:T(8,128)(2,1)}, u32[]{:S(2)}) %copy-start.1) | copy-done | bytes 1048600
  3.4 0.0 copy-start.2
  3.4 1.2 %copy-done.2 = bf16[1024,512]{1,0:T(8,128)(2,1)S(1)} copy-done((bf16[1024,512]{1,0:T(8,128)(2,1)S(1)}, bf16[1024,512]{1,0:T(8,128)(2,1)}, u32[]{:S(2)}) %copy-start.2) | copy-done | bytes 1048600
  4.6 0.0 copy-start.3
  4.6 1.2 %copy-done.3 = bf16[512,1024]{1,0:T(8,128)(2,1)S(1)} copy-done((bf16[512,1024]{1,0:T(8,128)(2,1)S(1)}, bf16[512,1024]{1,0:T(8,128)(2,1)}, u32[]{:S(2)}) %copy-start.3) | copy-done | bytes 1048600
  5.9 0.0 copy-start.4
  5.9 0.9 %copy-done.4 = bf16[192,512]{1,0:T(8,128)(2,1)S(1)} copy-done((bf16[192,512]{1,0:T(8,128)(2,1)S(1)}, bf16[192,512]{1,0:T(8,128)(2,1)}, u32[]{:S(2)}) %copy-start.4) | copy-done | bytes 196632
  6.8 0.0 copy-start.5
  6.8 0.9 %copy-done.5 = bf16[192,512]{1,0:T(8,128)(2,1)S(1)} copy-done((bf16[192,512]{1,0:T(8,128)(2,1)S(1)}, bf16[192,512]{1,0:T(8,128)(2,1)}, u32[]{:S(2)}) %copy-start.5) | copy-done | bytes 196632
  7.7 0.0 copy-start.6
  7.7 0.9 %copy-done.6 = bf16[192,512]{1,0:T(8,128)(2,1)S(1)} copy-done((bf16[192,512]{1,0:T(8,128)(2,1)S(1)}, bf16[192,512]{1,0:T(8,128)(2,1)}, u32[]{:S(2)}) %copy-start.6) | copy-done | bytes 196632
  8.7 0.0 copy-start.7
  8.7 0.9 %copy-done.7 = bf16[192,512]{1,0:T(8,128)(2,1)S(1)} copy-done((bf16[192,512]{1,0:T(8,128)(2,1)S(1)}, bf16[192,512]{1,0:T(8,128)(2,1)}, u32[]{:S(2)}) %copy-start.7) | copy-done | bytes 196632
  9.6 59.9 %shard_map.91 = bf16[192,512]{1,0:T(8,128)(2,1)S(1)} custom-call(s32[128]{0:T(128)S(1)} %broadcast_add_fusion.slot_ref, s32[96]{0:T(128)S(1)} %get-tuple-element.6.place_ref, bf16[6,32,512]{2,1,0:T(8,128)(2,1)S(1)} %bitcast.4, bf16[6,32,512]{2,1,0:T(8,128)(2,1)S(1)} %bitcast.5, bf16[6,32,512]{2,1,0:T(8,128)(2,1)S(1)} %bitcast.6, ...), custom_call_target="tpu_custom_call" | custom-call | tf_op jit(solution)/shard_map/pallas_call | solution.py:388
  69.5 0.7 copy.11
  (2 shorter events, 0.0 us)
Async XLA Ops:
  0.0 0.7 copy-start.8
  1.0 1.2 %copy-start = (bf16[1024,512]{1,0:T(8,128)(2,1)S(1)}, bf16[1024,512]{1,0:T(8,128)(2,1)}, u32[]{:S(2)}) copy-start(bf16[1024,512]{1,0:T(8,128)(2,1)} %wq_ref.1) | copy-start | bytes 3145732
  2.2 1.2 %copy-start.1 = (bf16[1024,512]{1,0:T(8,128)(2,1)S(1)}, bf16[1024,512]{1,0:T(8,128)(2,1)}, u32[]{:S(2)}) copy-start(bf16[1024,512]{1,0:T(8,128)(2,1)} %wk_ref.1) | copy-start | bytes 3145732
  3.4 1.2 %copy-start.2 = (bf16[1024,512]{1,0:T(8,128)(2,1)S(1)}, bf16[1024,512]{1,0:T(8,128)(2,1)}, u32[]{:S(2)}) copy-start(bf16[1024,512]{1,0:T(8,128)(2,1)} %wv_ref.1) | copy-start | bytes 3145732
  4.6 1.2 %copy-start.3 = (bf16[512,1024]{1,0:T(8,128)(2,1)S(1)}, bf16[512,1024]{1,0:T(8,128)(2,1)}, u32[]{:S(2)}) copy-start(bf16[512,1024]{1,0:T(8,128)(2,1)} %wo_ref.1) | copy-start | bytes 3145732
  5.9 0.9 %copy-start.4 = (bf16[192,512]{1,0:T(8,128)(2,1)S(1)}, bf16[192,512]{1,0:T(8,128)(2,1)}, u32[]{:S(2)}) copy-start(bf16[192,512]{1,0:T(8,128)(2,1)} %param.9) | copy-start | bytes 589828
  6.8 0.9 %copy-start.5 = (bf16[192,512]{1,0:T(8,128)(2,1)S(1)}, bf16[192,512]{1,0:T(8,128)(2,1)}, u32[]{:S(2)}) copy-start(bf16[192,512]{1,0:T(8,128)(2,1)} %param.10) | copy-start | bytes 589828
  7.7 0.9 %copy-start.6 = (bf16[192,512]{1,0:T(8,128)(2,1)S(1)}, bf16[192,512]{1,0:T(8,128)(2,1)}, u32[]{:S(2)}) copy-start(bf16[192,512]{1,0:T(8,128)(2,1)} %param.11) | copy-start | bytes 589828
  8.7 0.9 %copy-start.7 = (bf16[192,512]{1,0:T(8,128)(2,1)S(1)}, bf16[192,512]{1,0:T(8,128)(2,1)}, u32[]{:S(2)}) copy-start(bf16[192,512]{1,0:T(8,128)(2,1)} %param.12) | copy-start | bytes 589828

commit v2 on v1

--- a/solution.py
+++ b/solution.py
@@ -9,6 +9,9 @@
 
 HEAD_DIM = 128
 PAGE = 32
+CHUNKS = 2
+UNROLL = 2
+VMEM_GRANT = 67043328
 
 
 def per_device(queries, keys, values, out_grad, w_query, w_key, w_value, w_out, page_cluster):
@@ -143,7 +146,7 @@
 def whole_kernel(
     sizes, slot_ref, place_ref, q_ref, k_ref, v_ref, og_ref, wq_ref, wk_ref, wv_ref, wo_ref, out_ref,
     og_mine, og_other, wq_vm, wk_vm, wv_vm, wo_vm, grads, all_q, all_k, all_v, all_g,
-    slot_q, slot_k, slot_v, done_q, done_k, done_v, ret_q, ret_k, ret_v, part_out, part_in,
+    slot_q, slot_k, slot_v, done_q, done_k, done_v, ret_q, ret_k, ret_v, part_out, part_in, mine, held, value_sum,
     load_sem, swap_send, swap_recv, fwd_send, fwd_recv, ret_send, ret_recv,
 ):
     peers, pages, heads, slots = sizes
@@ -207,8 +210,8 @@
             def _():
                 remote.start()
 
-    for tensor in range(3):
-        send_forward(tensor)
+    send_forward(0)
+    send_forward(1)
 
     loads[0].wait()
     loads[1].wait()
@@ -219,97 +222,130 @@
     grad_sum = grad_sum + dot(og_other[...].reshape(rows, width), wo_vm[:, there], NT)
     grads[...] = grad_sum.astype(jnp.bfloat16).reshape(pages, PAGE, width)
     send_forward(3)
+    send_forward(2)
 
     slot_sets = (slot_q, slot_k, slot_v)
     done_sets = (done_q, done_k, done_v)
     ret_sets = (ret_q, ret_k, ret_v)
     cluster_rows = slots * PAGE
 
-    def give_back(tensor, head, peer):
-        piece = done_sets[tensor].at[pl.ds(peer * pages, pages)]
-        spot = ret_sets[tensor].at[:, :, pl.ds(head * HEAD_DIM, HEAD_DIM)]
-        local = pltpu.make_async_copy(piece, spot, ret_recv.at[tensor, head])
+    split = pages // CHUNKS
+
+    def give_back(tensor, chunk, head, peer):
+        piece = done_sets[tensor].at[pl.ds(peer * pages + chunk * split, split)]
+        spot = ret_sets[tensor].at[pl.ds(chunk * split, split), :, pl.ds(head * HEAD_DIM, HEAD_DIM)]
+        local = pltpu.make_async_copy(piece, spot, ret_recv.at[tensor, chunk, head])
         remote = pltpu.make_async_remote_copy(
-            src_ref=piece, dst_ref=spot, send_sem=ret_send.at[tensor, peer],
-            recv_sem=ret_recv.at[tensor, head], device_id={"tok": peer}, device_id_type=MESH,
+            src_ref=piece, dst_ref=spot, send_sem=ret_send.at[tensor, chunk, peer],
+            recv_sem=ret_recv.at[tensor, chunk, head], device_id={"tok": peer}, device_id_type=MESH,
         )
         return local, remote
 
-    def own_head(head):
-        for tensor in range(4):
+    def wait_tensor(tensor, head):
+        for peer in range(peers):
+            piece = sources[tensor].at[:, :, pl.ds(head * HEAD_DIM, HEAD_DIM)]
+            spot = fulls[tensor].at[pl.ds(peer * pages, pages)]
+            if peer == owners[head]:
+                pltpu.make_async_copy(piece, spot, fwd_recv.at[tensor, peer]).wait()
+            else:
+                pltpu.make_async_remote_copy(
+                    src_ref=piece, dst_ref=spot, send_sem=fwd_send.at[tensor, head],
+                    recv_sem=fwd_recv.at[tensor, peer], device_id={"tok": peer}, device_id_type=MESH,
+                ).wait_recv()
+
+    def gather(full, cluster):
+        return jnp.concatenate(
+            [full[slot_ref[cluster * slots + slot]] for slot in range(slots)], axis=0
+        )
+
+    def scatter(slot_set, cluster, value):
+        slot_set[pl.ds(cluster * slots, slots)] = value.astype(jnp.bfloat16).reshape(
+            slots, PAGE, HEAD_DIM
+        )
+
+    def every_cluster(step):
+        def body(index, carry):
+            for lane in range(UNROLL):
+                step(index * UNROLL + lane)
+            return carry
+
+        lax.fori_loop(0, peers // UNROLL, body, 0)
+
+    def reorder(tensors):
+        def body(peer, carry):
+            for inner in range(pages):
+                page = peer * pages + inner
+                place = place_ref[page]
+                for tensor in tensors:
+                    done_sets[tensor][page] = slot_sets[tensor][place]
+            return carry
+
+        lax.fori_loop(0, peers, body, 0)
+
+    def send_back(tensors, chunk, head):
+        for tensor in tensors:
             for peer in range(peers):
-                piece = sources[tensor].at[:, :, pl.ds(head * HEAD_DIM, HEAD_DIM)]
-                spot = fulls[tensor].at[pl.ds(peer * pages, pages)]
-                if peer == owners[head]:
-                    pltpu.make_async_copy(piece, spot, fwd_recv.at[tensor, peer]).wait()
-                else:
-                    pltpu.make_async_remote_copy(
-                        src_ref=piece, dst_ref=spot, send_sem=fwd_send.at[tensor, head],
-                        recv_sem=fwd_recv.at[tensor, peer], device_id={"tok": peer}, device_id_type=MESH,
-                    ).wait_recv()
-
-    for head in range(heads):
-        @pl.when(me == owners[head])
-        def _():
-            own_head(head)
-
-    is_owner = functools.reduce(lambda a, b: a | b, [me == owner for owner in owners])
-
-    @pl.when(is_owner)
-    def _():
-        row_index = lax.broadcasted_iota(jnp.int32, (cluster_rows, cluster_rows), 0)
-        col_index = lax.broadcasted_iota(jnp.int32, (cluster_rows, cluster_rows), 1)
-
-        def cluster_step(cluster, carry):
-            picks = [slot_ref[cluster * slots + slot] for slot in range(slots)]
-            query, key, value, grad = [
-                jnp.concatenate([full[pick] for pick in picks], axis=0) for full in fulls
-            ]
-            allowed = col_index <= row_index
-            score = jnp.where(allowed, dot(query, key, NT) * scale, -1e30)
-            row_max = jnp.max(score, axis=1, keepdims=True)
-            raised = jnp.where(allowed, jnp.exp(score - row_max), 0.0)
-            weights = raised * (1.0 / jnp.sum(raised, axis=1, keepdims=True))
-            grad_weights = dot(grad, value, NT)
-            row_delta = jnp.sum(weights * grad_weights, axis=1, keepdims=True)
-            grad_score = (weights * (grad_weights - row_delta)).astype(jnp.bfloat16)
-            dquery = dot(grad_score, key, (((1,), (0,)), ((), ()))) * scale
-            dkey = dot(grad_score, query, TN) * scale
-            dvalue = dot(weights.astype(jnp.bfloat16), grad, TN)
-            spot = pl.ds(cluster * slots, slots)
-            shape = (slots, PAGE, HEAD_DIM)
-            slot_q[spot] = dquery.astype(jnp.bfloat16).reshape(shape)
-            slot_k[spot] = dkey.astype(jnp.bfloat16).reshape(shape)
-            slot_v[spot] = dvalue.astype(jnp.bfloat16).reshape(shape)
-            return carry
-
-        lax.fori_loop(0, peers, cluster_step, 0)
-
-        def page_step(page, carry):
-            place = place_ref[page]
-            for slot_set, done_set in zip(slot_sets, done_sets):
-                done_set[page] = slot_set[place]
-            return carry
-
-        lax.fori_loop(0, peers * pages, page_step, 0)
-
-    def send_back(head):
-        for peer in range(peers):
-            for tensor in range(3):
-                local, remote = give_back(tensor, head, peer)
+                local, remote = give_back(tensor, chunk, head, peer)
                 if peer == owners[head]:
                     local.start()
                 else:
                     remote.start()
 
-    for head in range(heads):
-        @pl.when(me == owners[head])
-        def _():
-            send_back(head)
-
-    for tensor in range(3):
+    def weigh(cluster):
+        query, key = gather(all_q, cluster), gather(all_k, cluster)
+        row_index = lax.broadcasted_iota(jnp.int32, (cluster_rows, cluster_rows), 0)
+        col_index = lax.broadcasted_iota(jnp.int32, (cluster_rows, cluster_rows), 1)
+        score = jnp.where(col_index <= row_index, dot(query, key, NT) * scale, -1e30)
+        row_max = jnp.max(score, axis=1, keepdims=True)
+        raised = jnp.exp(score - row_max)
+        held[cluster] = raised * (1.0 / jnp.sum(raised, axis=1, keepdims=True))
+
+    def value_step(cluster):
+        scatter(slot_v, cluster, dot(held[cluster].astype(jnp.bfloat16), gather(all_g, cluster), TN))
+
+    def score_step(cluster):
+        query, key, value, grad = [gather(full, cluster) for full in fulls]
+        weights = held[cluster]
+        grad_weights = dot(grad, value, NT)
+        row_delta = jnp.sum(weights * grad_weights, axis=1, keepdims=True)
+        grad_score = (weights * (grad_weights - row_delta)).astype(jnp.bfloat16)
+        scatter(slot_q, cluster, dot(grad_score, key, (((1,), (0,)), ((), ()))) * scale)
+        scatter(slot_k, cluster, dot(grad_score, query, TN) * scale)
+
+    def as_owner(todo):
         for head in range(heads):
-            local, remote = give_back(tensor, head, owners[head])
+            @pl.when(me == owners[head])
+            def _():
+                todo(head)
+
+    is_owner = functools.reduce(lambda a, b: a | b, [me == owner for owner in owners])
+
+    as_owner(lambda head: (wait_tensor(0, head), wait_tensor(1, head)))
+
+    @pl.when(is_owner)
+    def _():
+        every_cluster(weigh)
+
+    as_owner(lambda head: wait_tensor(3, head))
+
+    @pl.when(is_owner)
+    def _():
+        every_cluster(value_step)
+        reorder((2,))
+
+    as_owner(lambda head: [send_back((2,), chunk, head) for chunk in range(CHUNKS)])
+    as_owner(lambda head: wait_tensor(2, head))
+
+    @pl.when(is_owner)
+    def _():
+        every_cluster(score_step)
+        reorder((0, 1))
+
+    as_owner(lambda head: [send_back((0, 1), chunk, head) for chunk in range(CHUNKS)])
+
+    def wait_back(tensor, chunk):
+        for head in range(heads):
+            local, remote = give_back(tensor, chunk, head, owners[head])
 
             @pl.when(me == owners[head])
             def _():
@@ -321,23 +357,38 @@
 
     for load in loads[2:]:
         load.wait()
-    grads_in = [ret[...].reshape(rows, width) for ret in ret_sets]
-    weights_in = (wq_vm, wk_vm, wv_vm)
-
-    def partial(half):
-        total = dot(grads_in[0], weights_in[0][half, :], NT)
-        total = total + dot(grads_in[1], weights_in[1][half, :], NT)
-        return (total + dot(grads_in[2], weights_in[2][half, :], NT)).astype(jnp.bfloat16)
-
-    part_out[...] = partial(there)
-    part_swap = pltpu.make_async_remote_copy(
-        src_ref=part_out, dst_ref=part_in, send_sem=swap_send.at[1], recv_sem=swap_recv.at[1],
-        device_id={"head": other}, device_id_type=MESH,
-    )
-    part_swap.start()
-    mine = partial(here).astype(jnp.float32)
-    part_swap.wait()
-    out_ref[...] = (mine + part_in[...].astype(jnp.float32)).astype(jnp.bfloat16)
+    chunk_rows = split * PAGE
+    for chunk in range(CHUNKS):
+        wait_back(2, chunk)
+    value_sum[...] = dot(ret_v[...].reshape(rows, width), wv_vm[...], NT)
+
+    swaps = []
+    for chunk in range(CHUNKS):
+        span = pl.ds(chunk * chunk_rows, chunk_rows)
+        wait_back(0, chunk)
+        wait_back(1, chunk)
+        dquery = ret_q[pl.ds(chunk * split, split)].reshape(chunk_rows, width)
+        dkey = ret_k[pl.ds(chunk * split, split)].reshape(chunk_rows, width)
+
+        def partial(half):
+            total = dot(dquery, wq_vm[half, :], NT) + dot(dkey, wk_vm[half, :], NT)
+            return (total + value_sum[span, half]).astype(jnp.bfloat16)
+
+        part_out[chunk] = partial(there)
+        swap = pltpu.make_async_remote_copy(
+            src_ref=part_out.at[chunk], dst_ref=part_in.at[chunk],
+            send_sem=swap_send.at[1 + chunk], recv_sem=swap_recv.at[1 + chunk],
+            device_id={"head": other}, device_id_type=MESH,
+        )
+        swap.start()
+        swaps.append(swap)
+        mine[span, :] = partial(here)
+    for chunk in range(CHUNKS):
+        span = pl.ds(chunk * chunk_rows, chunk_rows)
+        swaps[chunk].wait()
+        out_ref[span, :] = (
+            mine[span, :].astype(jnp.float32) + part_in[chunk].astype(jnp.float32)
+        ).astype(jnp.bfloat16)
 
     for head in range(heads):
         @pl.when(me != owners[head])
@@ -350,13 +401,15 @@
             for peer in range(peers):
                 if peer != owners[head]:
                     for tensor in range(3):
-                        give_back(tensor, head, peer)[1].wait_send()
+                        for chunk in range(CHUNKS):
+                            give_back(tensor, chunk, head, peer)[1].wait_send()
 
 
 def gathered_bytes(peers, rows, heads):
     tokens = peers * rows
     slot_rows = peers * (peers // 2) * PAGE
-    return (4 * tokens + 3 * slot_rows + 3 * tokens) * HEAD_DIM * 2
+    weights = peers * ((peers // 2) * PAGE) ** 2 * 4
+    return (7 * tokens + 3 * slot_rows) * HEAD_DIM * 2 + weights
 
 
 def per_device_fast(queries, keys, values, out_grad, w_query, w_key, w_value, w_out, page_cluster):
@@ -383,27 +436,32 @@
     done = pltpu.VMEM((page_total, PAGE, HEAD_DIM), half)
     small = pltpu.VMEM(paged, half)
     weight = pltpu.VMEM(w_query.shape, half)
-    any_space = pl.BlockSpec(memory_space=pl.ANY)
+    in_hbm = pl.BlockSpec(memory_space=pltpu.HBM)
     smem = pl.BlockSpec(memory_space=pltpu.SMEM)
     return pl.pallas_call(
         functools.partial(whole_kernel, (peers, pages, heads, slots)),
         out_shape=jax.ShapeDtypeStruct((rows, width), half),
-        in_specs=[smem, smem] + [any_space] * 8,
+        in_specs=[smem, smem] + [in_hbm] * 8,
         out_specs=pl.BlockSpec(memory_space=pltpu.VMEM),
         scratch_shapes=[small, small, weight, weight, weight, pltpu.VMEM(w_out.shape, half), small]
         + [full] * 4 + [slotted] * 3 + [done] * 3 + [small] * 3
-        + [pltpu.VMEM((rows, width), half)] * 2
+        + [pltpu.VMEM((CHUNKS, rows // CHUNKS, width), half)] * 2
+        + [
+            pltpu.VMEM((rows, width), half),
+            pltpu.VMEM((peers, slots * PAGE, slots * PAGE), jnp.float32),
+            pltpu.VMEM((rows, w_query.shape[0]), jnp.float32),
+        ]
         + [
             pltpu.SemaphoreType.DMA((5,)),
-            pltpu.SemaphoreType.DMA((2,)),
-            pltpu.SemaphoreType.DMA((2,)),
+            pltpu.SemaphoreType.DMA((1 + CHUNKS,)),
+            pltpu.SemaphoreType.DMA((1 + CHUNKS,)),
             pltpu.SemaphoreType.DMA((4, heads)),
             pltpu.SemaphoreType.DMA((4, peers)),
-            pltpu.SemaphoreType.DMA((3, peers)),
-            pltpu.SemaphoreType.DMA((3, heads)),
+            pltpu.SemaphoreType.DMA((3, CHUNKS, peers)),
+            pltpu.SemaphoreType.DMA((3, CHUNKS, heads)),
         ],
         compiler_params=pltpu.CompilerParams(
-            collective_id=0, has_side_effects=True, vmem_limit_bytes=40 * 1024 * 1024
+            collective_id=0, has_side_effects=True, vmem_limit_bytes=VMEM_GRANT
         ),
     )(
         slot_page, place, queries.reshape(paged), keys.reshape(paged), values.reshape(paged),
@@ -416,7 +474,8 @@
     heads = width // HEAD_DIM
     peers = lax.axis_size("tok")
     fits = gathered_bytes(peers, rows, heads) < 24 * 1024 * 1024
-    if lax.axis_size("head") == 2 and heads > 1 and (peers // 2) % heads == 0 and fits:
+    whole_chunks = (rows // PAGE) % CHUNKS == 0 and peers % UNROLL == 0
+    if lax.axis_size("head") == 2 and heads > 1 and (peers // 2) % heads == 0 and fits and whole_chunks:
         return per_device_fast(*arrays)
     return per_device(*arrays)
 

time: 70.5 us -> 54.4 us (0.77)
  the two profiles are of different devices: /device:TPU:13 before, /device:TPU:0 now
where the time goes in v2:
time: 54.4 us; the launch traced here: 54.3 us
  Pallas kernels  50.6 us (93%)
  local copies, waits for them, and re-layouts  2.84 us (5%)
  other arithmetic  0.8 us (1%)
    pallas_call x1, Pallas kernels, per_device_fast(): pl.pallas_call(functools.partial(whole_kernel, (peers, pages, heads, slot...  50.6 us
    unnamed x5, local copies, waits for them, and re-layouts  2.84 us

profile of v2, /device:TPU:0, one launch (start us, length us, event | category | flops | bytes accessed | tf_op | source)
XLA Modules:
  0.0 54.3 jit_solution(17488015338667638940)
XLA Ops:
  0.0 0.0 copy-start.1
  0.0 0.7 %copy-done.1 = s32[96]{0:T(128)S(1)} copy-done((s32[96]{0:T(128)S(1)}, s32[96]{0:T(128)}, u32[]{:S(2)}) %copy-start.1) | copy-done | bytes 408
  0.7 0.2 convert_reduce_fusion
  0.8 0.0 copy-start
  0.9 0.6 %copy-done = s32[96]{0:T(128)} copy-done((s32[96]{0:T(128)}, s32[96]{0:T(128)S(1)}, u32[]{:S(2)}) %copy-start) | copy-done | bytes 408
  1.4 0.1 select_reduce_fusion
  1.5 0.5 broadcast_add_fusion.slot_ref
  2.0 50.6 %shard_map.91 = bf16[192,512]{1,0:T(8,128)(2,1)} custom-call(s32[128]{0:T(128)} %broadcast_add_fusion.slot_ref, s32[96]{0:T(128)} %copy-done, bf16[6,32,512]{2,1,0:T(8,128)(2,1)} %bitcast.4, bf16[6,32,512]{2,1,0:T(8,128)(2,1)} %bitcast.5, bf16[6,32,512]{2,1,0:T(8,128)(2,1)} %bitcast.6, bf16[6,32,512]{2,1,0:T(8,128)(2,1)} %bitcast.7, ...), custom_call_target="tpu_custom_call" | custom-call | tf_op jit(solution)/shard_map/pallas_call | solution.py:441
  52.6 1.6 %copy.11 = bf16[192,512]{1,0:T(8,128)(2,1)} copy(bf16[192,512]{1,0:T(8,128)(2,1)} %shard_map.91) | data formatting | bytes 393216
  (1 shorter events, 0.0 us)
Async XLA Ops:
  0.0 0.7 %copy-start.1 = (s32[96]{0:T(128)S(1)}, s32[96]{0:T(128)}, u32[]{:S(2)}) copy-start(s32[96]{0:T(128)} %param.17) | copy-start | bytes 1156
  0.8 0.6 %copy-start = (s32[96]{0:T(128)}, s32[96]{0:T(128)S(1)}, u32[]{:S(2)}) copy-start(s32[96]{0:T(128)S(1)} %get-tuple-element.6.place_ref) | copy-start | bytes 1156

commit v3 on v2

--- a/solution.py
+++ b/solution.py
@@ -9,7 +9,7 @@
 
 HEAD_DIM = 128
 PAGE = 32
-CHUNKS = 2
+CHUNKS = 3
 UNROLL = 2
 VMEM_GRANT = 67043328
 
@@ -144,9 +144,10 @@
 
 
 def whole_kernel(
-    sizes, slot_ref, place_ref, q_ref, k_ref, v_ref, og_ref, wq_ref, wk_ref, wv_ref, wo_ref, out_ref,
+    sizes, cluster_ref, q_ref, k_ref, v_ref, og_ref, wq_ref, wk_ref, wv_ref, wo_ref, out_ref,
     og_mine, og_other, wq_vm, wk_vm, wv_vm, wo_vm, grads, all_q, all_k, all_v, all_g,
     slot_q, slot_k, slot_v, done_q, done_k, done_v, ret_q, ret_k, ret_v, part_out, part_in, mine, held, value_sum,
+    cluster_vm, slot_vm, place_vm, slot_sm, place_sm,
     load_sem, swap_send, swap_recv, fwd_send, fwd_recv, ret_send, ret_recv,
 ):
     peers, pages, heads, slots = sizes
@@ -165,19 +166,56 @@
         pltpu.make_async_copy(wk_ref, wk_vm, load_sem.at[3]),
         pltpu.make_async_copy(wv_ref, wv_vm, load_sem.at[4]),
     ]
+    cluster_load = pltpu.make_async_copy(cluster_ref, cluster_vm, load_sem.at[5])
+    cluster_load.start()
     for load in loads:
         load.start()
 
+    is_owner = functools.reduce(lambda a, b: a | b, [me == owner for owner in owners])
     barrier = pltpu.get_barrier_semaphore()
     pl.semaphore_signal(barrier, inc=1, device_id={"head": other}, device_id_type=MESH)
     for peer in range(peers):
-        @pl.when(me != peer)
+        meets = me != peer if peer in owners else is_owner & (me != peer)
+
+        @pl.when(meets)
         def _():
             pl.semaphore_signal(barrier, inc=1, device_id={"tok": peer}, device_id_type=MESH)
+
     zero_page = jnp.zeros((PAGE, HEAD_DIM), jnp.bfloat16)
     for full in (all_q, all_k, all_v, all_g):
         full[peers * pages] = zero_page
-    pl.semaphore_wait(barrier, peers)
+    cluster_load.wait()
+    page_total = peers * pages
+    square = (page_total, page_total)
+    down = lax.broadcasted_iota(jnp.int32, square, 0)
+    along = lax.broadcasted_iota(jnp.int32, square, 1)
+
+    def upright(row):
+        return jnp.sum(jnp.where(down == along, row, 0), axis=1, keepdims=True)
+
+    cluster_row = cluster_vm[...]
+    before = (upright(cluster_row) == cluster_row) & (down < along)
+    rank_row = jnp.sum(before.astype(jnp.int32), axis=0, keepdims=True)
+    place_row = cluster_row * slots + rank_row
+    place_vm[...] = place_row
+    shape = (page_total, peers * slots)
+    hit = upright(place_row) == lax.broadcasted_iota(jnp.int32, shape, 1)
+    missing = lax.broadcasted_iota(jnp.int32, shape, 0) - page_total
+    slot_vm[...] = page_total + jnp.sum(jnp.where(hit, missing, 0), axis=0, keepdims=True)
+    tables = [
+        pltpu.make_async_copy(slot_vm, slot_sm, load_sem.at[6]),
+        pltpu.make_async_copy(place_vm, place_sm, load_sem.at[7]),
+    ]
+    for table in tables:
+        table.start()
+
+    @pl.when(is_owner)
+    def _():
+        pl.semaphore_wait(barrier, peers)
+
+    @pl.when(jnp.logical_not(is_owner))
+    def _():
+        pl.semaphore_wait(barrier, heads + 1)
 
     og_swap = pltpu.make_async_remote_copy(
         src_ref=og_ref, dst_ref=og_other, send_sem=swap_send.at[0], recv_sem=swap_recv.at[0],
@@ -255,7 +293,7 @@
 
     def gather(full, cluster):
         return jnp.concatenate(
-            [full[slot_ref[cluster * slots + slot]] for slot in range(slots)], axis=0
+            [full[slot_sm[0, cluster * slots + slot]] for slot in range(slots)], axis=0
         )
 
     def scatter(slot_set, cluster, value):
@@ -275,7 +313,7 @@
         def body(peer, carry):
             for inner in range(pages):
                 page = peer * pages + inner
-                place = place_ref[page]
+                place = place_sm[0, page]
                 for tensor in tensors:
                     done_sets[tensor][page] = slot_sets[tensor][place]
             return carry
@@ -318,8 +356,8 @@
             def _():
                 todo(head)
 
-    is_owner = functools.reduce(lambda a, b: a | b, [me == owner for owner in owners])
-
+    for table in tables:
+        table.wait()
     as_owner(lambda head: (wait_tensor(0, head), wait_tensor(1, head)))
 
     @pl.when(is_owner)
@@ -333,8 +371,8 @@
         every_cluster(value_step)
         reorder((2,))
 
+    as_owner(lambda head: wait_tensor(2, head))
     as_owner(lambda head: [send_back((2,), chunk, head) for chunk in range(CHUNKS)])
-    as_owner(lambda head: wait_tensor(2, head))
 
     @pl.when(is_owner)
     def _():
@@ -419,16 +457,6 @@
     peers = lax.axis_size("tok")
     slots = peers // 2
     page_total = page_cluster.shape[0]
-    page_order = jnp.arange(page_total, dtype=jnp.int32)
-    same = page_cluster[:, None] == page_cluster[None, :]
-    earlier = page_order[None, :] < page_order[:, None]
-    rank = jnp.sum((same & earlier).astype(jnp.int32), axis=1)
-    place = page_cluster * slots + rank
-    slot_order = jnp.arange(peers * slots, dtype=jnp.int32)
-    hit = place[None, :] == slot_order[:, None]
-    slot_page = page_total + jnp.sum(
-        jnp.where(hit, page_order[None, :] - page_total, 0), axis=1
-    ).astype(jnp.int32)
     paged = (pages, PAGE, width)
     half = jnp.bfloat16
     full = pltpu.VMEM((page_total + 1, PAGE, HEAD_DIM), half)
@@ -437,11 +465,10 @@
     small = pltpu.VMEM(paged, half)
     weight = pltpu.VMEM(w_query.shape, half)
     in_hbm = pl.BlockSpec(memory_space=pltpu.HBM)
-    smem = pl.BlockSpec(memory_space=pltpu.SMEM)
     return pl.pallas_call(
         functools.partial(whole_kernel, (peers, pages, heads, slots)),
         out_shape=jax.ShapeDtypeStruct((rows, width), half),
-        in_specs=[smem, smem] + [in_hbm] * 8,
+        in_specs=[in_hbm] * 9,
         out_specs=pl.BlockSpec(memory_space=pltpu.VMEM),
         scratch_shapes=[small, small, weight, weight, weight, pltpu.VMEM(w_out.shape, half), small]
         + [full] * 4 + [slotted] * 3 + [done] * 3 + [small] * 3
@@ -451,8 +478,10 @@
             pltpu.VMEM((peers, slots * PAGE, slots * PAGE), jnp.float32),
             pltpu.VMEM((rows, w_query.shape[0]), jnp.float32),
         ]
+        + [pltpu.VMEM((1, size), jnp.int32) for size in (page_total, peers * slots, page_total)]
+        + [pltpu.SMEM((1, size), jnp.int32) for size in (peers * slots, page_total)]
         + [
-            pltpu.SemaphoreType.DMA((5,)),
+            pltpu.SemaphoreType.DMA((8,)),
             pltpu.SemaphoreType.DMA((1 + CHUNKS,)),
             pltpu.SemaphoreType.DMA((1 + CHUNKS,)),
             pltpu.SemaphoreType.DMA((4, heads)),
@@ -464,7 +493,7 @@
             collective_id=0, has_side_effects=True, vmem_limit_bytes=VMEM_GRANT
         ),
     )(
-        slot_page, place, queries.reshape(paged), keys.reshape(paged), values.reshape(paged),
+        page_cluster.reshape(1, page_total), queries.reshape(paged), keys.reshape(paged), values.reshape(paged),
         out_grad.reshape(paged), w_query, w_key, w_value, w_out,
     )
 

time: 54.4 us -> 51.1 us (0.939)
  Pallas kernels: 50.6 us -> 49.3 us
  local copies, waits for them, and re-layouts: 2.84 us -> 1.62 us
  other arithmetic: 0.8 us -> 0 us
    pallas_call x1, Pallas kernels: 50.6 us -> 49.3 us  [per_device_fast(): pl.pallas_call(functools.partial(whole_kernel, (peers, pages, heads, slot...]
    unnamed x5 -> x1, local copies, waits for them, and re-layouts: 2.84 us -> 1.62 us
where the time goes in v3:
time: 51.1 us; the launch traced here: 51 us
  Pallas kernels  49.3 us (96%)
  local copies, waits for them, and re-layouts  1.62 us (3%)
    pallas_call x1, Pallas kernels, per_device_fast(): pl.pallas_call(functools.partial(whole_kernel, (peers, pages, heads, slot...  49.3 us
    unnamed x1, local copies, waits for them, and re-layouts  1.62 us

profile of v3, /device:TPU:0, one launch (start us, length us, event | category | flops | bytes accessed | tf_op | source)
XLA Modules:
  0.0 51.0 jit_solution(5756219336430441774)
XLA Ops:
  0.0 49.3 %shard_map.91 = bf16[192,512]{1,0:T(8,128)(2,1)} custom-call(s32[1,96]{1,0:T(1,128)} %bitcast.9, bf16[6,32,512]{2,1,0:T(8,128)(2,1)} %bitcast.5, bf16[6,32,512]{2,1,0:T(8,128)(2,1)} %bitcast.6, bf16[6,32,512]{2,1,0:T(8,128)(2,1)} %bitcast.7, bf16[6,32,512]{2,1,0:T(8,128)(2,1)} %bitcast.8, bf16[1024,512]{1,0:T(8,128)(2,1)} %wq_ref.1, ...), custom_call_target="tpu_custom_call" | custom-call | tf_op jit(solution)/shard_map/pallas_call | solution.py:468
  49.3 1.6 %copy.11 = bf16[192,512]{1,0:T(8,128)(2,1)} copy(bf16[192,512]{1,0:T(8,128)(2,1)} %shard_map.91) | data formatting | bytes 393216

commit v4 on v3

--- a/solution.py
+++ b/solution.py
@@ -10,7 +10,7 @@
 HEAD_DIM = 128
 PAGE = 32
 CHUNKS = 3
-UNROLL = 2
+UNROLL = 4
 VMEM_GRANT = 67043328
 
 
@@ -237,7 +237,7 @@
         return local, remote
 
     def send_forward(tensor):
-        for head in range(heads):
+        for head in (0, 2, 1, 3):
             local, remote = forward(tensor, head)
 
             @pl.when(me == owners[head])
@@ -321,8 +321,8 @@
         lax.fori_loop(0, peers, body, 0)
 
     def send_back(tensors, chunk, head):
-        for tensor in tensors:
-            for peer in range(peers):
+        for peer in sorted(range(peers), key=lambda p: (p % 4, p // 4)):
+            for tensor in tensors:
                 local, remote = give_back(tensor, chunk, head, peer)
                 if peer == owners[head]:
                     local.start()

time: 51.1 us -> 49.8 us (0.975)
  Pallas kernels: 49.3 us -> 48 us
    pallas_call x1, Pallas kernels: 49.3 us -> 48 us  [per_device_fast(): pl.pallas_call(functools.partial(whole_kernel, (peers, pages, heads, slot...]
where the time goes in v4:
time: 49.8 us; the launch traced here: 49.7 us
  Pallas kernels  48 us (96%)
  local copies, waits for them, and re-layouts  1.62 us (3%)
    pallas_call x1, Pallas kernels, per_device_fast(): pl.pallas_call(functools.partial(whole_kernel, (peers, pages, heads, slot...  48 us
    unnamed x1, local copies, waits for them, and re-layouts  1.62 us

profile of v4, /device:TPU:0, one launch (start us, length us, event | category | flops | bytes accessed | tf_op | source)
XLA Modules:
  0.0 49.7 jit_solution(10921400639920430022)
XLA Ops:
  0.0 48.0 %shard_map.91 = bf16[192,512]{1,0:T(8,128)(2,1)} custom-call(s32[1,96]{1,0:T(1,128)} %bitcast.9, bf16[6,32,512]{2,1,0:T(8,128)(2,1)} %bitcast.5, bf16[6,32,512]{2,1,0:T(8,128)(2,1)} %bitcast.6, bf16[6,32,512]{2,1,0:T(8,128)(2,1)} %bitcast.7, bf16[6,32,512]{2,1,0:T(8,128)(2,1)} %bitcast.8, bf16[1024,512]{1,0:T(8,128)(2,1)} %wq_ref.1, ...), custom_call_target="tpu_custom_call" | custom-call | tf_op jit(solution)/shard_map/pallas_call | solution.py:468
  48.0 1.6 %copy.11 = bf16[192,512]{1,0:T(8,128)(2,1)} copy(bf16[192,512]{1,0:T(8,128)(2,1)} %shard_map.91) | data formatting | bytes 393216

commit v5 on v4

--- a/solution.py
+++ b/solution.py
@@ -237,7 +237,7 @@
         return local, remote
 
     def send_forward(tensor):
-        for head in (0, 2, 1, 3):
+        for head in sorted(range(heads), key=lambda head: head % 2):
             local, remote = forward(tensor, head)
 
             @pl.when(me == owners[head])
@@ -321,7 +321,7 @@
         lax.fori_loop(0, peers, body, 0)
 
     def send_back(tensors, chunk, head):
-        for peer in sorted(range(peers), key=lambda p: (p % 4, p // 4)):
+        for peer in sorted(range(peers), key=lambda peer: (peer % heads, -abs(peer - owners[head]))):
             for tensor in tensors:
                 local, remote = give_back(tensor, chunk, head, peer)
                 if peer == owners[head]:

time: 49.8 us -> 49.8 us (level)
  no operation moved by 1% of the time
where the time goes in v5:
time: 49.8 us; the launch traced here: 49.7 us
  Pallas kernels  48 us (96%)
  local copies, waits for them, and re-layouts  1.62 us (3%)
    pallas_call x1, Pallas kernels, per_device_fast(): pl.pallas_call(functools.partial(whole_kernel, (peers, pages, heads, slot...  48 us
    unnamed x1, local copies, waits for them, and re-layouts  1.62 us

profile of v5, /device:TPU:0, one launch (start us, length us, event | category | flops | bytes accessed | tf_op | source)
XLA Modules:
  0.0 49.7 jit_solution(6555700230894565676)
XLA Ops:
  0.0 48.0 %shard_map.91 = bf16[192,512]{1,0:T(8,128)(2,1)} custom-call(s32[1,96]{1,0:T(1,128)} %bitcast.9, bf16[6,32,512]{2,1,0:T(8,128)(2,1)} %bitcast.5, bf16[6,32,512]{2,1,0:T(8,128)(2,1)} %bitcast.6, bf16[6,32,512]{2,1,0:T(8,128)(2,1)} %bitcast.7, bf16[6,32,512]{2,1,0:T(8,128)(2,1)} %bitcast.8, bf16[1024,512]{1,0:T(8,128)(2,1)} %wq_ref.1, ...), custom_call_target="tpu_custom_call" | custom-call | tf_op jit(solution)/shard_map/pallas_call | solution.py:468
  48.0 1.6 %copy.11 = bf16[192,512]{1,0:T(8,128)(2,1)} copy(bf16[192,512]{1,0:T(8,128)(2,1)} %shard_map.91) | data formatting | bytes 393216
